TPU v7x, 256 devices: a whole 4x4x8 slice. The times are simulated.
256 devices in a mesh: row: 16 (over y, z_lo, core), col: 16 (over z_hi, x).
Axes of the slice: x: 4, y: 4, z: 8 (z_hi: 4, z_lo: 2; z = z_hi * 2 + z_lo), core: 2. Of those that a mesh axis runs over, the one named last changes fastest.
Arguments:
- tokens: bfloat16 [4096, 8192], P('col', 'row'), may hold values from -6 to 6
- grad_out: bfloat16 [4096, 16384], P('row', 'col'), may hold values from -6 to 6
- base_weight: float32 [8192, 16384], P('row', 'col'), may hold values from -6 to 6
- left_param: float32 [16, 512, 512], P('row'), may hold values from -6 to 6
- right_param: float32 [64, 256, 256], P('col'), may hold values from -6 to 6
Outputs:
- rotated_weight: float32 [8192, 16384], P('row', 'col')
- new_left: float32 [16, 512, 512], P('row')
- new_right: float32 [64, 256, 256], P('col')
All inputs are finite; a program needn't handle non-finite values.
Results may differ from a plain program's by a relative error of at most 0.0003.
Values may be sent and summed in bfloat16 or wider, within the bound.
A program may use at most 128 MiB of HBM per device.

v0:
```python
import math
import jax
import jax.numpy as jnp
from jax import lax
from jax.sharding import PartitionSpec as P

precise = lax.Precision.HIGHEST
taylor_degree = 6
step_rate = 0.3
epsilon = 1e-06


def batch_product(first, second):
    return jnp.einsum("lab,lbc->lac", first, second, precision=precise)


def transpose_last(matrix):
    return jnp.swapaxes(matrix, 1, 2)


def skew_from(param):
    skew_scale = 0.5 / math.sqrt(param.shape[-1])
    return skew_scale * (param - transpose_last(param))


def column_levels(skew, col_start, col_width):
    dimension = skew.shape[-1]
    eye_part = (
        jnp.arange(dimension)[:, None] == col_start + jnp.arange(col_width)[None, :]
    ).astype(jnp.float32)
    current = (
        eye_part[None] + lax.dynamic_slice_in_dim(skew, col_start, col_width, 2) / taylor_degree
    )
    horner_levels = [current] * (taylor_degree + 1)
    for divisor in range(taylor_degree - 1, 0, -1):
        current = eye_part[None] + batch_product(skew, current) / divisor
        horner_levels[divisor] = current
    return horner_levels


def adjoint(skew, horner_levels, upper_grad):
    running = jnp.zeros(skew.shape, jnp.float32)
    for divisor in range(1, taylor_degree):
        running = (
            running
            + batch_product(upper_grad, transpose_last(horner_levels[divisor + 1])) / divisor
        )
        upper_grad = batch_product(transpose_last(skew), upper_grad) / divisor
    return (running, upper_grad)


def update_param(param, accum):
    skew_scale = 0.5 / math.sqrt(param.shape[-1])
    grad_param = skew_scale * (accum - transpose_last(accum))
    root_mean = jnp.sqrt(jnp.mean(grad_param * grad_param, axis=(1, 2), keepdims=True) + epsilon)
    return param - step_rate * grad_param / root_mean


def right_apply(weight, rotation):
    count = rotation.shape[0]
    block = rotation.shape[-1]
    shaped = weight.reshape(weight.shape[0], count, block)
    return jnp.einsum("nbr,brs->nbs", shaped, rotation, precision=precise).reshape(weight.shape)


def body(tokens, grad_out, base_weight, left_param, right_param):
    col_count = lax.axis_size("col")
    left_size = left_param.shape[-1]
    left_count = left_param.shape[0]
    right_size = right_param.shape[-1]
    right_count = right_param.shape[0]
    row_total = base_weight.shape[0]
    col_total = base_weight.shape[1]
    col_width = left_size // col_count
    col_start = lax.axis_index("col") * col_width
    left_skew = skew_from(left_param)
    right_skew = skew_from(right_param)
    left_cols = column_levels(left_skew, col_start, col_width)
    right_levels = column_levels(right_skew, 0, right_size)
    right_rot = right_levels[1]
    token_all = lax.all_gather(tokens, "col", axis=0, tiled=True)
    left_rot = lax.all_gather(left_cols[1], "col", axis=2, tiled=True)
    grads_all = lax.all_gather(grad_out, "row", axis=0, tiled=True)
    grad_weight = lax.dot_general(
        token_all, grads_all, (((0,), (0,)), ((), ())), preferred_element_type=jnp.float32
    )
    weight_blocks = base_weight.reshape(left_count, left_size, col_total)
    grad_blocks = grad_weight.reshape(left_count, left_size, col_total)
    mixed_weight = right_apply(base_weight, right_rot).reshape(left_count, left_size, col_total)
    left_part = jnp.einsum("lnc,lmc->lnm", grad_blocks, mixed_weight, precision=precise)
    rotated = batch_product(left_rot, weight_blocks).reshape(row_total, right_count, right_size)
    right_part = jnp.einsum(
        "nbr,nbs->brs",
        rotated,
        grad_weight.reshape(row_total, right_count, right_size),
        precision=precise,
    )
    right_grad = lax.psum(right_part, "row")
    upper_piece = lax.psum_scatter(left_part, "col", scatter_dimension=2, tiled=True)
    partial_sum, upper_piece = adjoint(left_skew, left_cols, upper_piece)
    placed = lax.dynamic_update_slice_in_dim(
        jnp.zeros_like(partial_sum), upper_piece / taylor_degree, col_start, 2
    )
    left_acc = lax.psum(partial_sum + placed, "col")
    right_acc, right_upper = adjoint(right_skew, right_levels, right_grad)
    right_acc = right_acc + right_upper / taylor_degree
    new_left = update_param(left_param, left_acc)
    new_right = update_param(right_param, right_acc)
    new_left_skew = skew_from(new_left)
    new_cols = column_levels(new_left_skew, col_start, col_width)[1]
    new_left_rot = lax.all_gather(new_cols, "col", axis=2, tiled=True)
    new_right_rot = column_levels(skew_from(new_right), 0, right_size)[1]
    turned = batch_product(new_left_rot, weight_blocks).reshape(row_total, col_total)
    rotated_weight = right_apply(turned, new_right_rot)
    return (rotated_weight, new_left, new_right)


def solution(mesh):
    return jax.shard_map(
        body,
        mesh=mesh,
        in_specs=(
            P("col", "row"),
            P("row", "col"),
            P("row", "col"),
            P("row", None, None),
            P("col", None, None),
        ),
        out_specs=(P("row", "col"), P("row", None, None), P("col", None, None)),
        check_vma=False,
    )
```

profile of v0, /device:TPU:8, one launch (start us, length us, event | category | flops | bytes accessed | tf_op | source)
XLA Modules:
  0.0 776.7 jit_solution(18041137845352495483)
XLA Ops:
  31.0 5.0 fusion
  36.1 52.4 %all-gather.7.cloned.1.call-done = bf16[4096,512]{1,0:T(8,128)(2,1)} async-done(((bf16[256,512]{1,0:T(8,128)(2,1)}), bf16[4096,512]{1,0:T(8,128)(2,1)}) %all-gather.7.cloned.1.call-update) | async-done | bytes 4194320 | tf_op jit(solution)/shard_map/all_gather | solution.py:81
  88.4 56.7 %all-gather.9.cloned.1.call-done = bf16[4096,1024]{1,0:T(8,128)(2,1)} async-done(((bf16[256,1024]{1,0:T(8,128)(2,1)}), bf16[4096,1024]{1,0:T(8,128)(2,1)}) %all-gather.9.cloned.1.call-update) | async-done | bytes 8388624 | tf_op jit(solution)/shard_map/all_gather | solution.py:83
  145.1 8.3 %fusion.122 = f32[512,1024]{1,0:T(8,128)S(1)} fusion(bf16[4096,512]{1,0:T(8,128)(2,1)} %all-gather.7.cloned.1.call-done, bf16[4096,1024]{1,0:T(8,128)(2,1)} %all-gather.9.cloned.1.call-done), kind=kOutput, calls=%fused_computation.176 | convolution fusion | flops 4294967296 | bytes 14680064 | tf_op jit(solution)/shard_map/dot_general | solution.py:84
  154.8 4.5 convolution_bitcast_fusion
  159.3 3.6 copy.45
  162.9 39.3 %all-gather.11.cloned.1.call-done = f32[512,512]{0,1:T(8,128)} async-done(((f32[512,32]{0,1:T(8,128)}), f32[512,512]{0,1:T(8,128)}) %all-gather.11.cloned.1.call-update) | async-done | bytes 1048592 | tf_op jit(solution)/shard_map/all_gather | solution.py:82
  202.2 5.5 fusion.7
  207.8 3.1 fusion.2
  212.6 158.8 %all-reduce.9.cloned.1.call-done = f32[1,512,512]{1,0,2:T(1,128)} async-done(((f32[1,512,512]{1,0,2:T(1,128)}), f32[1,512,512]{1,0,2:T(1,128)}) %all-reduce.9.cloned.1.call-update) | async-done | bytes 1048592
  373.9 2.8 fusion.84
  376.7 116.3 %all-reduce.5.cloned.1.call-done = f32[4,256,256]{2,1,0:T(8,128)} async-done(((f32[4,256,256]{2,1,0:T(8,128)}), f32[4,256,256]{2,1,0:T(8,128)}) %all-reduce.5.cloned.1.call-update) | async-done | bytes 1048592 | tf_op jit(solution)/shard_map/psum | solution.py:98
  493.0 2.4 fusion.78
  503.7 2.2 fusion.22
  516.4 3.0 fusion.21
  519.3 2.2 fusion.20
  525.9 165.5 %all-reduce.7.cloned.1.call-done = f32[1,512,512]{1,2,0:T(8,128)} async-done(((f32[1,512,512]{1,2,0:T(8,128)}), f32[1,512,512]{1,2,0:T(8,128)}) %all-reduce.7.cloned.1.call-update) | async-done | bytes 1048592 | tf_op jit(solution)/shard_map/psum | solution.py:104
  691.4 2.6 copy.46
  694.1 3.0 multiply_reduce_fusion
  697.8 2.5 copy.47
  716.6 2.9 convolution_add_fusion.1
  719.5 40.1 %all-gather.13.cloned.1.call-done = f32[512,512]{0,1:T(8,128)} async-done(((f32[512,32]{0,1:T(8,128)}), f32[512,512]{0,1:T(8,128)}) %all-gather.13.cloned.1.call-update) | async-done | bytes 1048592 | tf_op jit(solution)/shard_map/all_gather | solution.py:111
  759.6 4.7 fusion.5
  764.4 3.5 fusion.124
  (131 shorter events, 69.5 us)
Async XLA Ops:
  7.2 3.1 copy-start.2
  7.2 81.3 %all-gather.7.cloned.1.call-start = ((), (), s32[]{:S(2)}) async-start(), calls=%async_computation | async-start | bytes 4456448 | tf_op jit(solution)/shard_map/all_gather | solution.py:81
  7.9 137.2 %all-gather.9.cloned.1.call-start = ((), (), s32[]{:S(2)}) async-start(), calls=%async_computation.1 | async-start | bytes 8912896 | tf_op jit(solution)/shard_map/all_gather | solution.py:83
  8.7 193.5 %all-gather.11.cloned.1.call-start = ((), (), s32[]{:S(2)}) async-start(), calls=%async_computation.4 | async-start | bytes 1114112 | tf_op jit(solution)/shard_map/all_gather | solution.py:82
  12.0 4.3 copy-start.3
  12.8 2.1 copy-start.26
  14.9 356.4 %all-reduce.9.cloned.1.call-start = ((), (), s32[]{:S(2)}) async-start(), calls=%async_computation.6 | async-start | bytes 2097152
  23.3 1.9 copy-start.12
  145.1 9.7 %copy-start.19 = (f32[4,256,512]{2,1,0:T(8,128)S(1)}, f32[4,256,512]{2,1,0:T(8,128)}, u32[]{:S(2)}) copy-start(f32[4,256,512]{2,1,0:T(8,128)} %fusion) | copy-start | bytes 6291460
  162.9 330.1 %all-reduce.5.cloned.1.call-start = ((), (), s32[]{:S(2)}) async-start(), calls=%async_computation.2 | async-start | bytes 2097152 | tf_op jit(solution)/shard_map/psum | solution.py:98
  202.2 5.6 copy-start.18
  207.7 3.6 copy-start.30
  210.9 480.6 %all-reduce.7.cloned.1.call-start = ((), (), s32[]{:S(2)}) async-start(), calls=%async_computation.3 | async-start | bytes 2097152 | tf_op jit(solution)/shard_map/psum | solution.py:104
  497.8 2.2 copy-start.6
  497.8 2.2 copy-start.22
  503.6 2.2 copy-start.29
  505.8 3.4 copy-start.24
  505.8 3.4 copy-start.27
  516.3 3.0 copy-start.8
  516.3 243.3 %all-gather.13.cloned.1.call-start = ((), (), s32[]{:S(2)}) async-start(), calls=%async_computation.5 | async-start | bytes 1114112 | tf_op jit(solution)/shard_map/all_gather | solution.py:111
  691.4 2.6 copy-start.25
  704.2 2.9 copy-start.4
  716.6 43.0 %copy-start.1 = (f32[512,1024]{1,0:T(8,128)S(1)}, f32[512,1024]{1,0:T(8,128)}, u32[]{:S(2)}) copy-start(f32[512,1024]{1,0:T(8,128)} %param.7) | copy-start | bytes 6291460
  719.5 44.9 %copy-start.23 = (f32[4,256,256]{2,1,0:T(8,128)S(1)}, f32[4,256,256]{2,1,0:T(8,128)}, u32[]{:S(2)}) copy-start(f32[4,256,256]{2,1,0:T(8,128)} %convolution_add_fusion.1) | copy-start | bytes 3145732
  (14 other events, 18.5 us)
Sparse Core Ops, SparseCore 0:
  10.4 77.9 all-gather.6
  90.3 54.8 all-gather.8
  147.6 54.5 all-gather.10
  204.7 166.6 all-reduce.8
  374.4 118.5 all-reduce.4
  516.4 174.9 all-reduce.6
  707.2 52.3 all-gather.12
where the time goes:
time: 781 us; the launch traced here: 777 us
  waiting for transfers between devices  631 us (81%)
  matrix products  95.4 us (12%)
  local copies, waits for them, and re-layouts  25.2 us (3%)
  between operations  16.4 us (2%)
  other arithmetic  8.11 us (1%)
    psum x1, waiting for transfers between devices, body(): left_acc = lax.psum(partial_sum + placed, 'col')  166 us
    unnamed x8, waiting for transfers between devices  160 us
    psum x1, waiting for transfers between devices, body(): right_grad = lax.psum(right_part, 'row')  116 us
    dot_general x42, matrix products, batch_product(): return jnp.einsum('lab,lbc->lac', first, second, precision=precise)  71 us
    all_gather x1, waiting for transfers between devices, body(): grads_all = lax.all_gather(grad_out, 'row', axis=0, tiled=True)  56.7 us
    all_gather x1, waiting for transfers between devices, body(): token_all = lax.all_gather(tokens, 'col', axis=0, tiled=True)  52.4 us
    all_gather x1, waiting for transfers between devices, body(): new_left_rot = lax.all_gather(new_cols, 'col', axis=2, tiled=True)  40.1 us
    all_gather x1, waiting for transfers between devices, body(): left_rot = lax.all_gather(left_cols[1], 'col', axis=2, tiled=True)  39.3 us
  transfers between devices with their start and end apart: 7, of which 7 were waited for; matrix products, arithmetic and copies ran while one was open for 10% of the time, Pallas kernels for 0%

commit v1 on v0

--- a/solution.py
+++ b/solution.py
@@ -79,7 +79,11 @@
     right_levels = column_levels(right_skew, 0, right_size)
     right_rot = right_levels[1]
     token_all = lax.all_gather(tokens, "col", axis=0, tiled=True)
-    left_rot = lax.all_gather(left_cols[1], "col", axis=2, tiled=True)
+    part = left_cols[1]
+    size = lax.axis_size("col")
+    pieces = jnp.stack([part for _ in range(size)])
+    pieces = lax.all_to_all(pieces, "col", split_axis=0, concat_axis=0)
+    left_rot = jnp.concatenate(pieces, axis=2)
     grads_all = lax.all_gather(grad_out, "row", axis=0, tiled=True)
     grad_weight = lax.dot_general(
         token_all, grads_all, (((0,), (0,)), ((), ())), preferred_element_type=jnp.float32

time: 781 us -> 745 us (0.954)
  waiting for transfers between devices: 631 us -> 584 us
  starting transfers between devices: 1.15 us -> 12.4 us
    all_gather x1 -> x0, waiting for transfers between devices: 39.3 us -> none  [body(): left_rot = lax.all_gather(left_cols[1], 'col', axis=2, tiled=True)]
    all_to_all x0 -> x1, starting transfers between devices: none -> 11.1 us  [body(): pieces = lax.all_to_all(pieces, 'col', split_axis=0, concat_axis=0)]
    psum x1, waiting for transfers between devices: 116 us -> 107 us  [body(): right_grad = lax.psum(right_part, 'row')]
    all_gather x1, waiting for transfers between devices: 52.4 us -> 60.4 us  [body(): token_all = lax.all_gather(tokens, 'col', axis=0, tiled=True)]
    unnamed x8 -> x7, waiting for transfers between devices: 160 us -> 159 us
  transfers between devices with their start and end apart: 7 -> 7, of which waited for: 7 -> 6; matrix products, arithmetic and copies ran while one was open for 10% -> 13% of each run, Pallas kernels for 0% -> 0%
where the time goes in v1:
time: 745 us; the launch traced here: 740 us
  waiting for transfers between devices  584 us (78%)
  matrix products  91.9 us (12%)
  local copies, waits for them, and re-layouts  27.1 us (4%)
  between operations  16.4 us (2%)
  starting transfers between devices  12.4 us (2%)
  other arithmetic  8.48 us (1%)
    psum x1, waiting for transfers between devices, body(): left_acc = lax.psum(partial_sum + placed, 'col')  160 us
    unnamed x7, waiting for transfers between devices  159 us
    psum x1, waiting for transfers between devices, body(): right_grad = lax.psum(right_part, 'row')  107 us
    dot_general x42, matrix products, batch_product(): return jnp.einsum('lab,lbc->lac', first, second, precision=precise)  67.4 us
    all_gather x1, waiting for transfers between devices, body(): token_all = lax.all_gather(tokens, 'col', axis=0, tiled=True)  60.4 us
    all_gather x1, waiting for transfers between devices, body(): grads_all = lax.all_gather(grad_out, 'row', axis=0, tiled=True)  56.7 us
    all_gather x1, waiting for transfers between devices, body(): new_left_rot = lax.all_gather(new_cols, 'col', axis=2, tiled=True)  40.1 us
  transfers between devices with their start and end apart: 7, of which 6 were waited for; matrix products, arithmetic and copies ran while one was open for 13% of the time, Pallas kernels for 0%

profile of v1, /device:TPU:8, one launch (start us, length us, event | category | flops | bytes accessed | tf_op | source)
XLA Modules:
  0.0 740.2 jit_solution(9288583220795203699)
XLA Ops:
  15.3 11.1 %all-to-all-start = ((f32[16,1,512,32]{2,3,1,0:T(8,128)}), f32[16,1,512,32]{2,3,1,0:T(8,128)}, u32[]{:S(2)}, u32[]{:S(2)}) async-start(f32[16,1,512,32]{2,3,1,0:T(8,128)} %stack.2), calls=%async_computation | async-start | bytes 2097152 | tf_op jit(solution)/shard_map/all_to_all | solution.py:85
  30.8 1.9 fusion.22
  41.6 5.0 fusion
  46.6 60.4 %all-gather.5.cloned.1.call-done = bf16[4096,512]{1,0:T(8,128)(2,1)} async-done(((bf16[256,512]{1,0:T(8,128)(2,1)}), bf16[4096,512]{1,0:T(8,128)(2,1)}) %all-gather.5.cloned.1.call-update) | async-done | bytes 4194320 | tf_op jit(solution)/shard_map/all_gather | solution.py:81
  107.0 56.7 %all-gather.7.cloned.1.call-done = bf16[4096,1024]{1,0:T(8,128)(2,1)} async-done(((bf16[256,1024]{1,0:T(8,128)(2,1)}), bf16[4096,1024]{1,0:T(8,128)(2,1)}) %all-gather.7.cloned.1.call-update) | async-done | bytes 8388624 | tf_op jit(solution)/shard_map/all_gather | solution.py:87
  163.7 8.3 %fusion.117 = f32[512,1024]{1,0:T(8,128)S(1)} fusion(bf16[4096,512]{1,0:T(8,128)(2,1)} %all-gather.5.cloned.1.call-done, bf16[4096,1024]{1,0:T(8,128)(2,1)} %all-gather.7.cloned.1.call-done), kind=kOutput, calls=%fused_computation.171 | convolution fusion | flops 4294967296 | bytes 14680064 | tf_op jit(solution)/shard_map/dot_general | solution.py:88
  173.4 4.5 convolution_bitcast_fusion
  177.9 3.6 copy.78
  181.6 2.9 copy.103
  185.8 5.5 fusion.116
  191.3 3.1 fusion.3
  194.7 157.7 %all-reduce.9.cloned.1.call-done = f32[1,512,512]{1,0,2:T(1,128)} async-done(((f32[1,512,512]{1,0,2:T(1,128)}), f32[1,512,512]{1,0,2:T(1,128)}) %all-reduce.9.cloned.1.call-update) | async-done | bytes 1048592
  366.9 107.2 %all-reduce.5.cloned.1.call-done = f32[4,256,256]{2,1,0:T(8,128)} async-done(((f32[4,256,256]{2,1,0:T(8,128)}), f32[4,256,256]{2,1,0:T(8,128)}) %all-reduce.5.cloned.1.call-update) | async-done | bytes 1048592 | tf_op jit(solution)/shard_map/psum | solution.py:102
  474.2 2.4 fusion.72
  491.3 160.4 %all-reduce.7.cloned.1.call-done = f32[1,512,512]{1,2,0:T(8,128)} async-done(((f32[1,512,512]{1,2,0:T(8,128)}), f32[1,512,512]{1,2,0:T(8,128)}) %all-reduce.7.cloned.1.call-update) | async-done | bytes 1048592 | tf_op jit(solution)/shard_map/psum | solution.py:108
  651.7 2.6 copy.79
  654.3 3.0 multiply_reduce_fusion
  658.0 2.5 copy.80
  668.9 1.9 fusion.13
  674.7 2.1 fusion.10
  676.8 2.9 convolution_add_fusion.1
  679.7 40.1 %all-gather.9.cloned.1.call-done = f32[512,512]{0,1:T(8,128)} async-done(((f32[512,32]{0,1:T(8,128)}), f32[512,512]{0,1:T(8,128)}) %all-gather.9.cloned.1.call-update) | async-done | bytes 1048592 | tf_op jit(solution)/shard_map/all_gather | solution.py:115
  719.9 7.9 %fusion.34 = f32[512,4,256]{2,0,1:T(8,128)S(1)} fusion(f32[4,256,512]{2,1,0:T(8,128)S(1)} %bitcast.150, f32[512,512]{0,1:T(8,128)} %all-gather.9.cloned.1.call-done), kind=kOutput, calls=%fused_computation.71 | convolution fusion | flops 3221225472 | bytes 5242880 | tf_op jit(solution)/shard_map/lab,lbc->lac/dot_general | solution.py:14
  727.8 3.5 fusion.119
  (126 shorter events, 66.4 us)
Async XLA Ops:
  7.2 3.1 copy-start.1
  7.2 99.9 %all-gather.5.cloned.1.call-start = ((), (), s32[]{:S(2)}) async-start(), calls=%async_computation.1 | async-start | bytes 4456448 | tf_op jit(solution)/shard_map/all_gather | solution.py:81
  7.9 155.8 %all-gather.7.cloned.1.call-start = ((), (), s32[]{:S(2)}) async-start(), calls=%async_computation.2 | async-start | bytes 8912896 | tf_op jit(solution)/shard_map/all_gather | solution.py:87
  12.7 2.6 copy-start.24
  13.5 1.9 copy-start.26
  14.2 13.6 %copy-start.2 = (f32[4,256,256]{2,1,0:T(8,128)S(1)}, f32[4,256,256]{2,1,0:T(8,128)}, u32[]{:S(2)}) copy-start(f32[4,256,256]{2,1,0:T(8,128)} %param.9) | copy-start | bytes 3145732
  15.3 170.4 %all-to-all-start = ((f32[16,1,512,32]{2,3,1,0:T(8,128)}), f32[16,1,512,32]{2,3,1,0:T(8,128)}, u32[]{:S(2)}, u32[]{:S(2)}) async-start(f32[16,1,512,32]{2,3,1,0:T(8,128)} %stack.2), calls=%async_computation | async-start | bytes 2097152 | tf_op jit(solution)/shard_map/all_to_all | solution.py:85
  26.4 326.0 %all-reduce.9.cloned.1.call-start = ((), (), s32[]{:S(2)}) async-start(), calls=%async_computation.6 | async-start | bytes 2097152
  29.1 1.7 copy-start.18
  32.8 1.9 copy-start.8
  34.8 3.9 copy-start.10
  36.7 4.9 copy-start.12
  39.6 1.9 copy-start.14
  163.7 9.7 %copy-start.17 = (f32[4,256,512]{2,1,0:T(8,128)S(1)}, f32[4,256,512]{2,1,0:T(8,128)}, u32[]{:S(2)}) copy-start(f32[4,256,512]{2,1,0:T(8,128)} %fusion) | copy-start | bytes 6291460
  181.5 292.6 %all-reduce.5.cloned.1.call-start = ((), (), s32[]{:S(2)}) async-start(), calls=%async_computation.3 | async-start | bytes 2097152 | tf_op jit(solution)/shard_map/psum | solution.py:102
  181.6 2.9 copy-start.27
  185.8 5.6 copy-start.16
  194.5 457.2 %all-reduce.7.cloned.1.call-start = ((), (), s32[]{:S(2)}) async-start(), calls=%async_computation.4 | async-start | bytes 2097152 | tf_op jit(solution)/shard_map/psum | solution.py:108
  353.2 5.1 copy-start.25
  366.5 353.4 %all-gather.9.cloned.1.call-start = ((), (), s32[]{:S(2)}) async-start(), calls=%async_computation.5 | async-start | bytes 1114112 | tf_op jit(solution)/shard_map/all_gather | solution.py:115
  651.7 2.6 copy-start.23
  664.5 2.9 copy-start.3
  676.8 43.0 %copy-start = (f32[1024,512]{1,0:T(8,128)S(1)}, f32[1024,512]{1,0:T(8,128)}, u32[]{:S(2)}) copy-start(f32[1024,512]{1,0:T(8,128)} %copy.103) | copy-start | bytes 6291460
  679.7 48.1 %copy-start.22 = (f32[4,256,256]{2,1,0:T(8,128)S(1)}, f32[4,256,256]{2,1,0:T(8,128)}, u32[]{:S(2)}) copy-start(f32[4,256,256]{2,1,0:T(8,128)} %convolution_add_fusion.1) | copy-start | bytes 3145732
  (11 other events, 12.9 us)
Sparse Core Ops, SparseCore 0:
  10.4 96.5 all-gather.4
  108.9 54.8 all-gather.6
  181.7 170.6 all-reduce.8
  355.5 118.6 all-reduce.4
  476.7 174.9 all-reduce.6
  667.4 52.3 all-gather.8
